TPU v7x, 512 devices: a whole 4x4x16 slice. The times are simulated.
512 devices in a mesh: bx: 16 (over x_lo, y, core), by: 32 (over z, x_hi).
Axes of the slice: x: 4 (x_hi: 2, x_lo: 2; x = x_hi * 2 + x_lo), y: 4, z: 16, core: 2. Of those that a mesh axis runs over, the one named last changes fastest.
Arguments:
- solution: float32 [4, 2048, 2048], P(None, 'by', 'bx'), may hold values from -6 to 6
- source: float32 [4, 2048, 2048], P(None, 'by', 'bx'), may hold values from -12 to 12
- class_ids: int32 [4, 2048, 2048], P(None, 'by', 'bx'), may hold values from 0 to 7
- conductivity: float32 [8], replicated, may hold values from 0.3 to 3
- spacing_x: float32 [2048], P('bx'), may hold values from 0.7 to 1.4
- spacing_y: float32 [2048], P('by'), may hold values from 0.7 to 1.4
- spacing_z: float32 [4], replicated, may hold values from 0.7 to 1.4
- forward_x: bfloat16 [2048, 2048], P('bx'), may hold values from -0.125 to 0.125
- forward_y: bfloat16 [2048, 2048], P('by'), may hold values from -0.125 to 0.125
- forward_z: bfloat16 [4, 4], replicated, may hold values from -3 to 3
- inverse_x: bfloat16 [2048, 2048], P('bx'), may hold values from -0.125 to 0.125
- inverse_y: bfloat16 [2048, 2048], P('by'), may hold values from -0.125 to 0.125
- inverse_z: bfloat16 [4, 4], replicated, may hold values from -3 to 3
- eigen_x: float32 [2048], P('bx'), may hold values from 0.05 to 4
- eigen_y: float32 [2048], P('by'), may hold values from 0.05 to 4
- eigen_z: float32 [4], replicated, may hold values from 0.05 to 4
Outputs:
- corrected: float32 [4, 2048, 2048], P(None, 'by', 'bx')
All inputs are finite; a program needn't handle non-finite values.
Results may differ from a plain program's by a relative error of at most 0.0039.
Values may be sent and summed in bfloat16 or wider, within the bound.
A program may use at most 64 MiB of HBM per device.

v0:
```python
import jax
import jax.numpy as jnp
from jax import lax
from jax.sharding import Mesh
from jax.sharding import PartitionSpec as P

CLASSES = 8
BY = ("by_0", "by_1")
shift_value = 0.1


def with_halo(value, sides, width):
    edges = {}
    for axis, dim in sides:
        size, length = (lax.axis_size(axis), value.shape[dim])
        up = [(i, (i + 1) % size) for i in range(size - 1)]
        last = lax.slice_in_dim(value, length - width, length, axis=dim)
        first = lax.slice_in_dim(value, 0, width, axis=dim)
        edges[dim] = (
            lax.ppermute(last, axis, up),
            lax.ppermute(first, axis, [(b, a) for a, b in up]),
        )
    done = []
    for _, dim in sides:
        low, high = edges[dim]
        around = [(width, width) if d in done else (0, 0) for d in range(value.ndim)]
        value = jnp.concatenate([jnp.pad(low, around), value, jnp.pad(high, around)], axis=dim)
        done.append(dim)
    return value


def whole_of(value, axes, dim):
    filled = value
    for number in range(len(axes) - 1, -1, -1):
        filled = lax.all_gather(filled, axes[number], axis=dim, tiled=True)
    return filled


def coefficients(class_ids, conductivity):
    result = jnp.zeros(class_ids.shape, jnp.float32)
    for index in range(CLASSES):
        result = result + jnp.where(class_ids == index, conductivity[index], jnp.float32(0.0))
    return result


def operate(solution, coef):
    stacked = jnp.stack([solution, coef])
    padded = with_halo(stacked, (("bx", 3), (BY, 2)), 1)
    padded = jnp.pad(padded, ((0, 0), (1, 1), (0, 0), (0, 0)))
    values = padded[0]
    padcoef = padded[1]
    slices = [
        (slice(2, None), slice(1, -1), slice(1, -1)),
        (slice(0, -2), slice(1, -1), slice(1, -1)),
        (slice(1, -1), slice(2, None), slice(1, -1)),
        (slice(1, -1), slice(0, -2), slice(1, -1)),
        (slice(1, -1), slice(1, -1), slice(2, None)),
        (slice(1, -1), slice(1, -1), slice(0, -2)),
    ]
    result = jnp.zeros(solution.shape, jnp.float32)
    for where_at in slices:
        neighbour = values[where_at]
        ncoef = padcoef[where_at]
        face = jnp.where(ncoef > 0, 2.0 * coef * ncoef / (coef + ncoef), coef)
        result = result + face * (solution - neighbour)
    return result


def x_high(values, matrix_rows):
    columns = matrix_rows.astype(jnp.float32)
    return jnp.einsum(
        "kjx,mx->kjm",
        lax.all_gather(values, "bx", axis=2, tiled=True),
        columns,
        precision=lax.Precision.HIGHEST,
    )


def y_low(values, matrix_rows):
    return jnp.einsum(
        "kjm,nj->knm", whole_of(values, BY, 1), matrix_rows, preferred_element_type=jnp.float32
    )


def on_device(
    solution,
    source,
    class_ids,
    conductivity,
    spacing_x,
    spacing_y,
    spacing_z,
    forward_x,
    forward_y,
    forward_z,
    inverse_x,
    inverse_y,
    inverse_z,
    eigen_x,
    eigen_y,
    eigen_z,
):
    highest = lax.Precision.HIGHEST
    coef = coefficients(class_ids, conductivity)
    operated = operate(solution, coef)
    weights = spacing_z[:, None, None] * spacing_y[None, :, None] * spacing_x[None, None, :]
    restricted = (weights * (source - operated)).astype(jnp.bfloat16)
    modes_xy = x_high(y_low(restricted, forward_y), forward_x)
    modes = jnp.einsum("qk,knm->qnm", forward_z.astype(jnp.float32), modes_xy, precision=highest)
    divisor = eigen_x[None, None, :] + eigen_y[None, :, None] + eigen_z[:, None, None] + shift_value
    scaled = modes / divisor
    spectral = jnp.einsum(
        "kq,qnm->knm", inverse_z.astype(jnp.float32), scaled, precision=highest
    ).astype(jnp.bfloat16)
    field = x_high(y_low(spectral, inverse_y), inverse_x)
    return solution + weights * field


def solution(mesh):
    split = Mesh(mesh.devices.reshape(mesh.shape["bx"], 16, 2), ("bx", "by_0", "by_1"))
    placed = (
        P(None, BY, "bx"),
        P(None, BY, "bx"),
        P(None, BY, "bx"),
        P(),
        P("bx"),
        P(BY),
        P(),
        P("bx", None),
        P(BY, None),
        P(),
        P("bx", None),
        P(BY, None),
        P(),
        P("bx"),
        P(BY),
        P(),
    )
    return jax.shard_map(
        on_device, mesh=split, in_specs=placed, out_specs=P(None, BY, "bx"), check_vma=False
    )
```

profile of v0, /device:TPU:1, one launch (start us, length us, event | category | flops | bytes accessed | tf_op | source)
XLA Modules:
  0.0 307.3 jit_solution(11412667438014760652)
XLA Ops:
  6.5 1.6 fusion.42
  8.2 6.0 %fusion.41 = f32[1,4,64,128]{3,2,1,0:T(8,128)S(1)} fusion(f32[]{:T(128)} %bitcast.8, s32[4,64,128]{2,1,0:T(8,128)} %param.18, f32[]{:T(128)} %bitcast.7, f32[]{:T(128)} %bitcast.6, f32[]{:T(128)} %bitcast.5, f32[]{:T(128)} %bitcast.4, f32[]{:T(128)} %bitcast.3, f32[]{:T(128)} %bitcast.2, f32[]{:T(128)} %bitcast.1), kind=kLoop, calls=%fused_computation.69 | loop fusion | flops 753664 | bytes 262176 | tf_op jit(solution)/shard_map/stack | solution.py:47
  14.2 1.1 fusion.14
  15.3 4.6 %collective-permute-start.1 = (f32[2,4,64,1]{3,2,1,0:T(8,128)S(1)}, f32[2,4,64,1]{3,2,1,0:T(8,128)S(1)}, u32[]{:S(2)}, u32[]{:S(2)}) collective-permute-start(f32[2,4,64,1]{3,2,1,0:T(8,128)S(1)} %get-tuple-element.7), channel_id=1, source_target_pairs={{0,32},{32,64},{64,96},{96,128},{128,160},{160,192},{192,224},{224... | collective-permute-start | bytes 6152 | tf_op jit(solution)/shard_map/ppermute | solution.py:20
  19.9 5.5 %collective-permute-start.2 = (f32[2,4,64,1]{3,2,1,0:T(8,128)S(1)}, f32[2,4,64,1]{3,2,1,0:T(8,128)S(1)}, u32[]{:S(2)}, u32[]{:S(2)}) collective-permute-start(f32[2,4,64,1]{3,2,1,0:T(8,128)S(1)} %get-tuple-element.8), channel_id=1, source_target_pairs={{32,0},{64,32},{96,64},{128,96},{160,128},{192,160},{224,192},{256... | collective-permute-start | bytes 6152 | tf_op jit(solution)/shard_map/ppermute | solution.py:21
  25.4 0.7 pad_maximum_fusion.1
  26.1 1.3 collective-permute-start
  27.4 1.3 collective-permute-start.3
  28.7 0.7 broadcast_multiply_fusion
  29.5 3.9 %collective-permute-done.3 = f32[2,4,1,128]{3,2,1,0:T(1,128)S(1)} collective-permute-done((f32[2,4,1,128]{3,2,1,0:T(1,128)S(1)}, f32[2,4,1,128]{3,2,1,0:T(1,128)S(1)}, u32[]{:S(2)}, u32[]{:S(2)}) %collective-permute-start.3) | collective-permute-done | bytes 4128 | tf_op jit(solution)/shard_map/ppermute | solution.py:21
  33.4 1.2 select_maximum_fusion
  34.7 0.1 fusion.11
  34.8 5.5 %fusion.17 = bf16[4,64,128]{2,1,0:T(8,128)(2,1)S(1)} fusion(f32[4,64,128]{2,1,0:T(8,128)S(1)} %copy-done.5, f32[4,64,128]{2,1,0:T(8,128)S(1)} %copy-done.1, f32[6,66,130]{2,1,0:T(8,128)S(1)} %get-tuple-element.6, f32[6,66,130]{2,1,0:T(8,128)S(1)} %get-tuple-element.5, f32[128]{0:T(128)S(1)} %copy-done.6, f32[4,64]{1,0:T(4,128)S(1)} %broadcast_multiply_fusion, ...), kind=kLoop, calls=%fused_computation.30 | loop fusion | flops 2457600 | bytes 2033184 | tf_op jit(solution)/shard_map/convert_element_type | solution.py:107
  40.3 5.4 %all_gather.18 = bf16[4,128,128]{2,1,0:T(8,128)(2,1)} all-gather(bf16[4,64,128]{2,1,0:T(8,128)(2,1)S(1)} %fusion.17), channel_id=1, replica_groups=mesh['bx'=16,'by_0'=16,'by_1'=2] {'by_1'}, dimensions={1}, use_global_device_ids=true | all-gather | bytes 196608 | tf_op jit(solution)/shard_map/all_gather | solution.py:35
  45.7 0.0 all-gather.5.cloned.1.call-update
  45.7 0.0 all-gather.7.cloned.1.call-start
  45.8 70.4 %all-gather.5.cloned.1.call-done = bf16[4,2048,128]{2,1,0:T(8,128)(2,1)} async-done(((bf16[4,128,128]{2,1,0:T(8,128)(2,1)}), bf16[4,2048,128]{2,1,0:T(8,128)(2,1)}) %all-gather.5.cloned.1.call-update) | async-done | bytes 2097168 | tf_op jit(solution)/shard_map/all_gather | solution.py:35
  116.2 2.7 convolution_bitcast_fusion
  118.9 0.0 all-gather.9.cloned.1.call-start
  119.0 0.1 broadcast_add_fusion
  119.1 50.9 %all-gather.7.cloned.1.call-done = f32[4,64,2048]{2,1,0:T(8,128)} async-done(((f32[4,64,128]{2,1,0:T(8,128)}), f32[4,64,2048]{2,1,0:T(8,128)}) %all-gather.7.cloned.1.call-update) | async-done | bytes 2097168 | tf_op jit(solution)/shard_map/all_gather | solution.py:73
  170.0 2.7 fusion.9
  172.7 0.3 fusion.6
  173.1 0.2 fusion.7
  173.3 5.4 %all_gather.21 = bf16[4,128,128]{2,0,1:T(4,128)(2,1)} all-gather(bf16[4,64,128]{2,0,1:T(4,128)(2,1)S(1)} %fusion.7), channel_id=1, replica_groups=mesh['bx'=16,'by_0'=16,'by_1'=2] {'by_1'}, dimensions={1}, use_global_device_ids=true | all-gather | bytes 196608 | tf_op jit(solution)/shard_map/all_gather | solution.py:35
  178.7 0.0 all-gather.9.cloned.1.call-update
  178.7 0.0 all-gather.11.cloned.1.call-start
  178.8 64.6 %all-gather.9.cloned.1.call-done = bf16[4,2048,128]{2,0,1:T(4,128)(2,1)} async-done(((bf16[4,128,128]{2,0,1:T(4,128)(2,1)}), bf16[4,2048,128]{2,0,1:T(4,128)(2,1)}) %all-gather.9.cloned.1.call-update) | async-done | bytes 2097168 | tf_op jit(solution)/shard_map/all_gather | solution.py:35
  243.4 2.7 fusion.2
  246.1 0.0 all-gather.11.cloned.1.call-update
  246.1 51.2 %all-gather.11.cloned.1.call-done = f32[4,64,2048]{2,1,0:T(8,128)} async-done(((f32[4,64,128]{2,1,0:T(8,128)}), f32[4,64,2048]{2,1,0:T(8,128)}) %all-gather.11.cloned.1.call-update) | async-done | bytes 2097168 | tf_op jit(solution)/shard_map/all_gather | solution.py:73
  297.4 3.3 %fusion.5 = f32[4,64,128]{2,1,0:T(8,128)} fusion(f32[4,64,128]{2,1,0:T(8,128)S(1)} %copy-done.1, f32[4,64,2048]{2,1,0:T(8,128)} %all-gather.11.cloned.1.call-done, bf16[128,2048]{1,0:T(8,128)(2,1)S(1)} %copy-done.2, f32[128]{0:T(128)S(1)} %copy-done.6, f32[4,64]{1,0:T(4,128)S(1)} %broadcast_multiply_fusion), kind=kOutput, calls=%fused_computation.5 | convolution fusion | flops 805404672 | bytes 2885120 | tf_op jit(solution)/shard_map/kjx,mx->kjm/dot_general | solution.py:71
  (31 shorter events, 0.1 us)
Async XLA Ops:
  6.5 163.5 %copy-start = (bf16[128,2048]{1,0:T(8,128)(2,1)S(1)}, bf16[128,2048]{1,0:T(8,128)(2,1)}, u32[]{:S(2)}) copy-start(bf16[128,2048]{1,0:T(8,128)(2,1)} %param.23) | copy-start | bytes 1572868
  6.5 109.7 %all-gather.5.cloned.1.call-start = ((), (), s32[]{:S(2)}) async-start(), calls=%async_computation | async-start | bytes 2228224 | tf_op jit(solution)/shard_map/all_gather | solution.py:35
  8.2 26.6 %copy-start.1 = (f32[4,64,128]{2,1,0:T(8,128)S(1)}, f32[4,64,128]{2,1,0:T(8,128)}, u32[]{:S(2)}) copy-start(f32[4,64,128]{2,1,0:T(8,128)} %param.16) | copy-start | bytes 393220
  8.2 26.6 %copy-start.3 = (s32[4,64,128]{2,1,0:T(8,128)S(1)}, s32[4,64,128]{2,1,0:T(8,128)}, u32[]{:S(2)}) copy-start(s32[4,64,128]{2,1,0:T(8,128)} %param.18) | copy-start | bytes 393220
  8.2 26.6 %copy-start.5 = (f32[4,64,128]{2,1,0:T(8,128)S(1)}, f32[4,64,128]{2,1,0:T(8,128)}, u32[]{:S(2)}) copy-start(f32[4,64,128]{2,1,0:T(8,128)} %param.17) | copy-start | bytes 393220
  8.2 26.6 %copy-start.6 = (f32[128]{0:T(128)S(1)}, f32[128]{0:T(128)}, u32[]{:S(2)}) copy-start(f32[128]{0:T(128)} %param.20) | copy-start | bytes 1540
  15.3 14.2 %collective-permute-start.1 = (f32[2,4,64,1]{3,2,1,0:T(8,128)S(1)}, f32[2,4,64,1]{3,2,1,0:T(8,128)S(1)}, u32[]{:S(2)}, u32[]{:S(2)}) collective-permute-start(f32[2,4,64,1]{3,2,1,0:T(8,128)S(1)} %get-tuple-element.7), channel_id=1, source_target_pairs={{0,32},{32,64},{64,96},{96,128},{128,160},{160,192},{192,224},{224... | collective-permute-start | bytes 6152 | tf_op jit(solution)/shard_map/ppermute | solution.py:20
  19.9 9.6 %collective-permute-start.2 = (f32[2,4,64,1]{3,2,1,0:T(8,128)S(1)}, f32[2,4,64,1]{3,2,1,0:T(8,128)S(1)}, u32[]{:S(2)}, u32[]{:S(2)}) collective-permute-start(f32[2,4,64,1]{3,2,1,0:T(8,128)S(1)} %get-tuple-element.8), channel_id=1, source_target_pairs={{32,0},{64,32},{96,64},{128,96},{160,128},{192,160},{224,192},{256... | collective-permute-start | bytes 6152 | tf_op jit(solution)/shard_map/ppermute | solution.py:21
  26.1 3.3 %collective-permute-start = (f32[2,4,1,128]{3,2,1,0:T(1,128)S(1)}, f32[2,4,1,128]{3,2,1,0:T(1,128)S(1)}, u32[]{:S(2)}, u32[]{:S(2)}) collective-permute-start(f32[2,4,1,128]{3,2,1,0:T(1,128)S(1)} %get-tuple-element.9), channel_id=1, source_target_pairs={{0,1},{1,2},{2,3},{3,4},{4,5},{5,6},{6,7},{7,8},{8,9},{9,10},{10,1... | collective-permute-start | bytes 12296 | tf_op jit(solution)/shard_map/ppermute | solution.py:20
  27.4 6.0 %collective-permute-start.3 = (f32[2,4,1,128]{3,2,1,0:T(1,128)S(1)}, f32[2,4,1,128]{3,2,1,0:T(1,128)S(1)}, u32[]{:S(2)}, u32[]{:S(2)}) collective-permute-start(f32[2,4,1,128]{3,2,1,0:T(1,128)S(1)} %get-tuple-element.10), channel_id=1, source_target_pairs={{1,0},{2,1},{3,2},{4,3},{5,4},{6,5},{7,6},{8,7},{9,8},{10,9},{11,1... | collective-permute-start | bytes 12296 | tf_op jit(solution)/shard_map/ppermute | solution.py:21
  34.6 81.6 %copy-start.4 = (bf16[64,2048]{1,0:T(8,128)(2,1)S(1)}, bf16[64,2048]{1,0:T(8,128)(2,1)}, u32[]{:S(2)}) copy-start(bf16[64,2048]{1,0:T(8,128)(2,1)} %param.24) | copy-start | bytes 786436
  34.8 84.2 %copy-start.8 = (f32[64]{0:T(128)S(1)}, f32[64]{0:T(128)}, u32[]{:S(2)}) copy-start(f32[64]{0:T(128)} %param.30) | copy-start | bytes 772
  34.8 84.2 %copy-start.9 = (f32[128]{0:T(128)S(1)}, f32[128]{0:T(128)}, u32[]{:S(2)}) copy-start(f32[128]{0:T(128)} %param.29) | copy-start | bytes 1540
  45.7 127.0 %copy-start.11 = (bf16[4,4]{1,0:T(4,128)(2,1)S(1)}, bf16[4,4]{1,0:T(4,128)(2,1)}, u32[]{:S(2)}) copy-start(bf16[4,4]{1,0:T(4,128)(2,1)} %param.25) | copy-start | bytes 100
  45.7 127.0 %copy-start.12 = (f32[4]{0:T(128)S(1)}, f32[4]{0:T(128)}, u32[]{:S(2)}) copy-start(f32[4]{0:T(128)} %param.31) | copy-start | bytes 52
  45.7 124.3 %all-gather.7.cloned.1.call-start = ((), (), s32[]{:S(2)}) async-start(), calls=%async_computation.1 | async-start | bytes 2228224 | tf_op jit(solution)/shard_map/all_gather | solution.py:73
  118.9 54.1 %copy-start.7 = (bf16[4,4]{1,0:T(4,128)(2,1)S(1)}, bf16[4,4]{1,0:T(4,128)(2,1)}, u32[]{:S(2)}) copy-start(bf16[4,4]{1,0:T(4,128)(2,1)} %param.28) | copy-start | bytes 100
  118.9 124.4 %all-gather.9.cloned.1.call-start = ((), (), s32[]{:S(2)}) async-start(), calls=%async_computation.2 | async-start | bytes 2228224 | tf_op jit(solution)/shard_map/all_gather | solution.py:35
  119.1 124.3 %copy-start.10 = (bf16[64,2048]{1,0:T(8,128)(2,1)S(1)}, bf16[64,2048]{1,0:T(8,128)(2,1)}, u32[]{:S(2)}) copy-start(bf16[64,2048]{1,0:T(8,128)(2,1)} %param.27) | copy-start | bytes 786436
  172.7 124.7 %copy-start.2 = (bf16[128,2048]{1,0:T(8,128)(2,1)S(1)}, bf16[128,2048]{1,0:T(8,128)(2,1)}, u32[]{:S(2)}) copy-start(bf16[128,2048]{1,0:T(8,128)(2,1)} %param.26) | copy-start | bytes 1572868
  178.7 118.7 %all-gather.11.cloned.1.call-start = ((), (), s32[]{:S(2)}) async-start(), calls=%async_computation.3 | async-start | bytes 2228224 | tf_op jit(solution)/shard_map/all_gather | solution.py:73
Sparse Core Ops, SparseCore 0:
  45.8 70.3 all-gather.4
  119.1 50.8 all-gather.6
  178.8 64.4 all-gather.8
  246.3 51.0 all-gather.10
where the time goes:
time: 308 us; the launch traced here: 307 us
  waiting for transfers between devices  241 us (78%)
  other arithmetic  15.4 us (5%)
  between operations  13.4 us (4%)
  starting transfers between devices  12.8 us (4%)
  matrix products  12 us (4%)
  blocking collectives  10.8 us (4%)
    all_gather x2, waiting for transfers between devices, whole_of(): filled = lax.all_gather(filled, axes[number], axis=dim, tiled=True)  135 us
    all_gather x2, waiting for transfers between devices, x_high(): lax.all_gather(values, 'bx', axis=2, tiled=True)  102 us
    all_gather x2, blocking collectives, whole_of(): filled = lax.all_gather(filled, axes[number], axis=dim, tiled=True)  10.8 us
    another operation x2, other arithmetic, operate(): stacked = jnp.stack([solution, coef])  7.09 us
    ppermute x2, starting transfers between devices, with_halo(): lax.ppermute(first, axis, [(b, a) for a, b in up])  6.76 us
  transfers between devices with their start and end apart: 8, of which 5 were waited for; matrix products, arithmetic and copies ran while one was open for 1% of the time, Pallas kernels for 0%

commit v1 on v0

--- a/solution.py
+++ b/solution.py
@@ -3,10 +3,18 @@
 from jax import lax
 from jax.sharding import Mesh
 from jax.sharding import PartitionSpec as P
+from jax.lax import all_to_all, axis_size
 
 CLASSES = 8
 BY = ("by_0", "by_1")
 shift_value = 0.1
+
+
+def set_vector(z):
+    vec_out = axis_size("bx")
+    z_new = jnp.stack(vec_out * [z], axis=0)
+    finding = all_to_all(z_new, "bx", 0, 0)
+    return jnp.concatenate(finding, 2)
 
 
 def with_halo(value, sides, width):
@@ -68,12 +76,7 @@
 
 def x_high(values, matrix_rows):
     columns = matrix_rows.astype(jnp.float32)
-    return jnp.einsum(
-        "kjx,mx->kjm",
-        lax.all_gather(values, "bx", axis=2, tiled=True),
-        columns,
-        precision=lax.Precision.HIGHEST,
-    )
+    return jnp.einsum("kjx,mx->kjm", set_vector(values), columns, precision=lax.Precision.HIGHEST)
 
 
 def y_low(values, matrix_rows):

time: 308 us -> 285 us (0.925)
  waiting for transfers between devices: 241 us -> 164 us
  blocking collectives: 10.8 us -> 52.3 us
  starting transfers between devices: 12.8 us -> 27.7 us
  matrix products: 12 us -> 7.57 us
    all_gather x2 -> x0, waiting for transfers between devices: 102 us -> none  [x_high(): lax.all_gather(values, 'bx', axis=2, tiled=True)]
    all_to_all x0 -> x1, blocking collectives: none -> 41.5 us  [set_vector(): finding = all_to_all(z_new, 'bx', 0, 0)]
    all_to_all x0 -> x1, waiting for transfers between devices: none -> 27.4 us  [set_vector(): finding = all_to_all(z_new, 'bx', 0, 0)]
    all_to_all x0 -> x1, starting transfers between devices: none -> 15.1 us  [set_vector(): finding = all_to_all(z_new, 'bx', 0, 0)]
    dot_general x2, matrix products: 6 us -> 2.85 us  [x_high(): jnp.einsum('kjx,mx->kjm', set_vector(values), columns, precision=lax.Prec...]
  transfers between devices with their start and end apart: 8 -> 7, of which waited for: 5 -> 4; matrix products, arithmetic and copies ran while one was open for 1% -> 1% of each run, Pallas kernels for 0% -> 0%
where the time goes in v1:
time: 285 us
  waiting for transfers between devices  164 us (58%)
  blocking collectives  52.3 us (18%)
  starting transfers between devices  27.7 us (10%)
  other arithmetic  15.6 us (5%)
  between operations  13.6 us (5%)
  matrix products  7.57 us (3%)
  local copies, waits for them, and re-layouts  3.6 us (1%)
    all_gather x2, waiting for transfers between devices, whole_of(): filled = lax.all_gather(filled, axes[number], axis=dim, tiled=True)  133 us
    all_to_all x1, blocking collectives, set_vector(): finding = all_to_all(z_new, 'bx', 0, 0)  41.5 us
    all_to_all x1, waiting for transfers between devices, set_vector(): finding = all_to_all(z_new, 'bx', 0, 0)  27.4 us
    all_to_all x1, starting transfers between devices, set_vector(): finding = all_to_all(z_new, 'bx', 0, 0)  15.1 us
    all_gather x2, blocking collectives, whole_of(): filled = lax.all_gather(filled, axes[number], axis=dim, tiled=True)  10.8 us
    another operation x2, other arithmetic, operate(): stacked = jnp.stack([solution, coef])  7.24 us
    ppermute x2, starting transfers between devices, with_halo(): lax.ppermute(first, axis, [(b, a) for a, b in up])  6.76 us
    ppermute x2, starting transfers between devices, with_halo(): lax.ppermute(last, axis, up)  5.86 us
  transfers between devices with their start and end apart: 7, of which 4 were waited for; matrix products, arithmetic and copies ran while one was open for 1% of the time, Pallas kernels for 0%

profile of v1, /device:TPU:1, one launch (start us, length us, event | category | flops | bytes accessed | tf_op | source)
XLA Modules:
  0.0 284.6 jit_solution(11281936773659554815)
XLA Ops:
  6.5 1.6 fusion.52
  8.2 6.1 %fusion.51 = f32[1,4,64,128]{3,2,1,0:T(8,128)S(1)} fusion(f32[]{:T(128)} %bitcast.8, s32[4,64,128]{2,1,0:T(8,128)} %param.18, f32[]{:T(128)} %bitcast.7, f32[]{:T(128)} %bitcast.6, f32[]{:T(128)} %bitcast.5, f32[]{:T(128)} %bitcast.4, f32[]{:T(128)} %bitcast.3, f32[]{:T(128)} %bitcast.2, f32[]{:T(128)} %bitcast.1), kind=kLoop, calls=%fused_computation.74 | loop fusion | flops 753664 | bytes 262176 | tf_op jit(solution)/shard_map/stack | solution.py:55
  14.3 1.1 fusion.24
  15.5 4.6 %collective-permute-start.1 = (f32[2,4,64,1]{3,2,1,0:T(8,128)S(1)}, f32[2,4,64,1]{3,2,1,0:T(8,128)S(1)}, u32[]{:S(2)}, u32[]{:S(2)}) collective-permute-start(f32[2,4,64,1]{3,2,1,0:T(8,128)S(1)} %get-tuple-element.7), channel_id=1, source_target_pairs={{0,32},{32,64},{64,96},{96,128},{128,160},{160,192},{192,224},{224... | collective-permute-start | bytes 6152 | tf_op jit(solution)/shard_map/ppermute | solution.py:28
  20.1 5.5 %collective-permute-start.2 = (f32[2,4,64,1]{3,2,1,0:T(8,128)S(1)}, f32[2,4,64,1]{3,2,1,0:T(8,128)S(1)}, u32[]{:S(2)}, u32[]{:S(2)}) collective-permute-start(f32[2,4,64,1]{3,2,1,0:T(8,128)S(1)} %get-tuple-element.8), channel_id=1, source_target_pairs={{32,0},{64,32},{96,64},{128,96},{160,128},{192,160},{224,192},{256... | collective-permute-start | bytes 6152 | tf_op jit(solution)/shard_map/ppermute | solution.py:29
  25.5 0.7 pad_maximum_fusion.1
  26.3 1.3 collective-permute-start
  27.6 1.3 collective-permute-start.3
  28.9 0.7 broadcast_multiply_fusion
  29.6 3.9 %collective-permute-done.3 = f32[2,4,1,128]{3,2,1,0:T(1,128)S(1)} collective-permute-done((f32[2,4,1,128]{3,2,1,0:T(1,128)S(1)}, f32[2,4,1,128]{3,2,1,0:T(1,128)S(1)}, u32[]{:S(2)}, u32[]{:S(2)}) %collective-permute-start.3) | collective-permute-done | bytes 4128 | tf_op jit(solution)/shard_map/ppermute | solution.py:29
  33.6 1.2 select_maximum_fusion
  34.8 0.1 fusion.21
  34.9 5.6 %fusion.27 = bf16[4,64,128]{2,1,0:T(8,128)(2,1)S(1)} fusion(f32[4,64,128]{2,1,0:T(8,128)S(1)} %copy-done.5, f32[4,64,128]{2,1,0:T(8,128)S(1)} %copy-done.1, f32[6,66,130]{2,1,0:T(8,128)S(1)} %get-tuple-element.6, f32[6,66,130]{2,1,0:T(8,128)S(1)} %get-tuple-element.5, f32[128]{0:T(128)S(1)} %copy-done.6, f32[4,64]{1,0:T(4,128)S(1)} %broadcast_multiply_fusion, ...), kind=kLoop, calls=%fused_computation.35 | loop fusion | flops 2457600 | bytes 2033184 | tf_op jit(solution)/shard_map/convert_element_type | solution.py:110
  40.5 5.4 %all_gather.12 = bf16[4,128,128]{2,1,0:T(8,128)(2,1)} all-gather(bf16[4,64,128]{2,1,0:T(8,128)(2,1)S(1)} %fusion.27), channel_id=1, replica_groups=mesh['bx'=16,'by_0'=16,'by_1'=2] {'by_1'}, dimensions={1}, use_global_device_ids=true | all-gather | bytes 196608 | tf_op jit(solution)/shard_map/all_gather | solution.py:43
  45.9 0.0 all-gather.3.cloned.1.call-update
  45.9 70.5 %all-gather.3.cloned.1.call-done = bf16[4,2048,128]{2,1,0:T(8,128)(2,1)} async-done(((bf16[4,128,128]{2,1,0:T(8,128)(2,1)}), bf16[4,2048,128]{2,1,0:T(8,128)(2,1)}) %all-gather.3.cloned.1.call-update) | async-done | bytes 2097168 | tf_op jit(solution)/shard_map/all_gather | solution.py:43
  116.5 2.1 convolution_bitcast_fusion
  118.5 1.6 stack.13
  120.1 15.1 %all-to-all-start = ((f32[16,4,64,128]{3,2,1,0:T(8,128)}), f32[16,4,64,128]{3,2,1,0:T(8,128)S(1)}, u32[]{:S(2)}, u32[]{:S(2)}) async-start(f32[16,4,64,128]{3,2,1,0:T(8,128)} %stack.13), calls=%async_computation | async-start | bytes 4194304 | tf_op jit(solution)/shard_map/all_to_all | solution.py:16
  135.2 0.0 all-gather.5.cloned.1.call-start
  135.3 0.1 broadcast_add_fusion
  135.4 27.4 %all-to-all-done = f32[16,4,64,128]{3,2,1,0:T(8,128)S(1)} async-done(((f32[16,4,64,128]{3,2,1,0:T(8,128)}), f32[16,4,64,128]{3,2,1,0:T(8,128)S(1)}, u32[]{:S(2)}, u32[]{:S(2)}) %all-to-all-start) | async-done | bytes 2097184 | tf_op jit(solution)/shard_map/all_to_all | solution.py:16
  162.8 1.1 fusion.3
  163.9 0.3 fusion.17
  164.3 0.2 fusion.18
  164.5 5.4 %all_gather.14 = bf16[4,128,128]{2,0,1:T(4,128)(2,1)} all-gather(bf16[4,64,128]{2,0,1:T(4,128)(2,1)S(1)} %fusion.18), channel_id=1, replica_groups=mesh['bx'=16,'by_0'=16,'by_1'=2] {'by_1'}, dimensions={1}, use_global_device_ids=true | all-gather | bytes 196608 | tf_op jit(solution)/shard_map/all_gather | solution.py:43
  169.9 0.0 all-gather.5.cloned.1.call-update
  169.9 62.2 %all-gather.5.cloned.1.call-done = bf16[4,2048,128]{2,0,1:T(4,128)(2,1)} async-done(((bf16[4,128,128]{2,0,1:T(4,128)(2,1)}), bf16[4,2048,128]{2,0,1:T(4,128)(2,1)}) %all-gather.5.cloned.1.call-update) | async-done | bytes 2097168 | tf_op jit(solution)/shard_map/all_gather | solution.py:43
  232.2 2.1 fusion.8
  234.2 0.2 stack.14
  234.5 41.5 %all_to_all.10 = f32[16,4,64,128]{3,2,1,0:T(8,128)S(1)} all-to-all(f32[16,4,64,128]{3,2,1,0:T(8,128)S(1)} %stack.14), channel_id=1, replica_groups=mesh['bx'=16,'by_0'=16,'by_1'=2] {'bx'}, dimensions={0} | all-to-all | bytes 4194304 | tf_op jit(solution)/shard_map/all_to_all | solution.py:16
  276.0 1.8 fusion.14
  (30 shorter events, 0.1 us)
Async XLA Ops:
  6.5 156.2 %copy-start = (bf16[128,2048]{1,0:T(8,128)(2,1)S(1)}, bf16[128,2048]{1,0:T(8,128)(2,1)}, u32[]{:S(2)}) copy-start(bf16[128,2048]{1,0:T(8,128)(2,1)} %param.23) | copy-start | bytes 1572868
  6.5 109.9 %all-gather.3.cloned.1.call-start = ((), (), s32[]{:S(2)}) async-start(), calls=%async_computation.2 | async-start | bytes 2228224 | tf_op jit(solution)/shard_map/all_gather | solution.py:43
  8.2 26.7 %copy-start.1 = (f32[4,64,128]{2,1,0:T(8,128)S(1)}, f32[4,64,128]{2,1,0:T(8,128)}, u32[]{:S(2)}) copy-start(f32[4,64,128]{2,1,0:T(8,128)} %param.16) | copy-start | bytes 393220
  8.2 26.7 %copy-start.3 = (s32[4,64,128]{2,1,0:T(8,128)S(1)}, s32[4,64,128]{2,1,0:T(8,128)}, u32[]{:S(2)}) copy-start(s32[4,64,128]{2,1,0:T(8,128)} %param.18) | copy-start | bytes 393220
  8.2 26.7 %copy-start.5 = (f32[4,64,128]{2,1,0:T(8,128)S(1)}, f32[4,64,128]{2,1,0:T(8,128)}, u32[]{:S(2)}) copy-start(f32[4,64,128]{2,1,0:T(8,128)} %param.17) | copy-start | bytes 393220
  8.2 26.7 %copy-start.6 = (f32[128]{0:T(128)S(1)}, f32[128]{0:T(128)}, u32[]{:S(2)}) copy-start(f32[128]{0:T(128)} %param.20) | copy-start | bytes 1540
  15.5 14.2 %collective-permute-start.1 = (f32[2,4,64,1]{3,2,1,0:T(8,128)S(1)}, f32[2,4,64,1]{3,2,1,0:T(8,128)S(1)}, u32[]{:S(2)}, u32[]{:S(2)}) collective-permute-start(f32[2,4,64,1]{3,2,1,0:T(8,128)S(1)} %get-tuple-element.7), channel_id=1, source_target_pairs={{0,32},{32,64},{64,96},{96,128},{128,160},{160,192},{192,224},{224... | collective-permute-start | bytes 6152 | tf_op jit(solution)/shard_map/ppermute | solution.py:28
  20.1 9.6 %collective-permute-start.2 = (f32[2,4,64,1]{3,2,1,0:T(8,128)S(1)}, f32[2,4,64,1]{3,2,1,0:T(8,128)S(1)}, u32[]{:S(2)}, u32[]{:S(2)}) collective-permute-start(f32[2,4,64,1]{3,2,1,0:T(8,128)S(1)} %get-tuple-element.8), channel_id=1, source_target_pairs={{32,0},{64,32},{96,64},{128,96},{160,128},{192,160},{224,192},{256... | collective-permute-start | bytes 6152 | tf_op jit(solution)/shard_map/ppermute | solution.py:29
  26.3 3.3 %collective-permute-start = (f32[2,4,1,128]{3,2,1,0:T(1,128)S(1)}, f32[2,4,1,128]{3,2,1,0:T(1,128)S(1)}, u32[]{:S(2)}, u32[]{:S(2)}) collective-permute-start(f32[2,4,1,128]{3,2,1,0:T(1,128)S(1)} %get-tuple-element.9), channel_id=1, source_target_pairs={{0,1},{1,2},{2,3},{3,4},{4,5},{5,6},{6,7},{7,8},{8,9},{9,10},{10,1... | collective-permute-start | bytes 12296 | tf_op jit(solution)/shard_map/ppermute | solution.py:28
  27.6 6.0 %collective-permute-start.3 = (f32[2,4,1,128]{3,2,1,0:T(1,128)S(1)}, f32[2,4,1,128]{3,2,1,0:T(1,128)S(1)}, u32[]{:S(2)}, u32[]{:S(2)}) collective-permute-start(f32[2,4,1,128]{3,2,1,0:T(1,128)S(1)} %get-tuple-element.10), channel_id=1, source_target_pairs={{1,0},{2,1},{3,2},{4,3},{5,4},{6,5},{7,6},{8,7},{9,8},{10,9},{11,1... | collective-permute-start | bytes 12296 | tf_op jit(solution)/shard_map/ppermute | solution.py:29
  34.8 81.7 %copy-start.4 = (bf16[64,2048]{1,0:T(8,128)(2,1)S(1)}, bf16[64,2048]{1,0:T(8,128)(2,1)}, u32[]{:S(2)}) copy-start(bf16[64,2048]{1,0:T(8,128)(2,1)} %param.24) | copy-start | bytes 786436
  120.1 15.1 %copy-start.8 = (f32[64]{0:T(128)S(1)}, f32[64]{0:T(128)}, u32[]{:S(2)}) copy-start(f32[64]{0:T(128)} %param.30) | copy-start | bytes 772
  120.1 15.1 %copy-start.9 = (f32[128]{0:T(128)S(1)}, f32[128]{0:T(128)}, u32[]{:S(2)}) copy-start(f32[128]{0:T(128)} %param.29) | copy-start | bytes 1540
  120.1 42.6 %all-to-all-start = ((f32[16,4,64,128]{3,2,1,0:T(8,128)}), f32[16,4,64,128]{3,2,1,0:T(8,128)S(1)}, u32[]{:S(2)}, u32[]{:S(2)}) async-start(f32[16,4,64,128]{3,2,1,0:T(8,128)} %stack.13), calls=%async_computation | async-start | bytes 4194304 | tf_op jit(solution)/shard_map/all_to_all | solution.py:16
  135.2 28.7 %copy-start.11 = (bf16[4,4]{1,0:T(4,128)(2,1)S(1)}, bf16[4,4]{1,0:T(4,128)(2,1)}, u32[]{:S(2)}) copy-start(bf16[4,4]{1,0:T(4,128)(2,1)} %param.25) | copy-start | bytes 100
  135.2 28.7 %copy-start.12 = (f32[4]{0:T(128)S(1)}, f32[4]{0:T(128)}, u32[]{:S(2)}) copy-start(f32[4]{0:T(128)} %param.31) | copy-start | bytes 52
  135.2 29.0 %copy-start.7 = (bf16[4,4]{1,0:T(4,128)(2,1)S(1)}, bf16[4,4]{1,0:T(4,128)(2,1)}, u32[]{:S(2)}) copy-start(bf16[4,4]{1,0:T(4,128)(2,1)} %param.28) | copy-start | bytes 100
  135.2 96.9 %all-gather.5.cloned.1.call-start = ((), (), s32[]{:S(2)}) async-start(), calls=%async_computation.3 | async-start | bytes 2228224 | tf_op jit(solution)/shard_map/all_gather | solution.py:43
  135.4 96.8 %copy-start.10 = (bf16[64,2048]{1,0:T(8,128)(2,1)S(1)}, bf16[64,2048]{1,0:T(8,128)(2,1)}, u32[]{:S(2)}) copy-start(bf16[64,2048]{1,0:T(8,128)(2,1)} %param.27) | copy-start | bytes 786436
  234.5 41.5 %copy-start.2 = (bf16[128,2048]{1,0:T(8,128)(2,1)S(1)}, bf16[128,2048]{1,0:T(8,128)(2,1)}, u32[]{:S(2)}) copy-start(bf16[128,2048]{1,0:T(8,128)(2,1)} %param.26) | copy-start | bytes 1572868
Sparse Core Ops, SparseCore 0:
  46.1 70.3 all-gather.2
  170.1 62.0 all-gather.4
